TPU v7x, 32 devices: a whole 2x2x4 slice. The times are simulated.
32 devices in a mesh: groups: 2 (over y), wide: 16 (over z, x, core).
Axes of the slice: x: 2, y: 2, z: 4, core: 2. Of those that a mesh axis runs over, the one named last changes fastest.
Arguments:
- fields: bfloat16 [32, 512], P(('groups', 'wide')), parts along dimension 0, may hold values from -6 to 6
- chol: bfloat16 [512, 1024, 1024], P(None, 'wide'), may hold values from -0.01171875 to 0.01171875
- orbitals: bfloat16 [32, 1024, 256], P(('groups', 'wide')), parts along dimension 0, may hold values from -6 to 6
- trial: bfloat16 [1024, 256], replicated, may hold values from -0.5 to 0.5
Outputs:
- new_orbitals: bfloat16 [32, 1024, 256], P(('groups', 'wide')), parts along dimension 0
- force_bias: float32 [32, 2, 512], P(('groups', 'wide')), parts along dimension 0
There are 2 independent parts, one for each index of `groups`. A program takes and returns all parts, laid end to end along the dimension named above; an argument that names none is the same for every part. Nothing has to cross between parts.
All inputs are finite; a program needn't handle non-finite values.
Results may differ from a plain program's by a relative error of at most 0.0075.
Values may be sent and summed in bfloat16 or wider, within the bound.
No kernel may reach another device: no remote copies, remote signals or barrier semaphores. Data moves between devices by JAX's collectives and lax.ppermute only.
A program may use at most 192 MiB of HBM per device.

v0:
```python
import jax
import jax.numpy as jnp
from jax import lax
from jax.sharding import PartitionSpec as P

TAYLOR = 4


def per_device(fields, chol, orbitals, trial):
    all_fields = lax.all_gather(fields, "wide", axis=0, tiled=True)
    vectors, rows, width = chol.shape
    chol_flat = chol.reshape(vectors, rows * width)
    generator = jnp.dot(all_fields, chol_flat, preferred_element_type=jnp.float32).astype(
        jnp.bfloat16
    )
    generator = generator.reshape(all_fields.shape[0], rows, width)
    owned = lax.all_to_all(generator, "wide", split_axis=0, concat_axis=1, tiled=True)
    nocc = orbitals.shape[2] // 2
    walk_local = orbitals.shape[0]
    gen_walker = owned[0]
    total = orbitals[0].astype(jnp.float32)
    operand = orbitals[0]
    for order in range(1, TAYLOR + 1):
        product = jnp.dot(gen_walker, operand, preferred_element_type=jnp.float32)
        term = jnp.concatenate([-product[:, nocc:], product[:, :nocc]], axis=1) / order
        total = total + term
        if order < TAYLOR:
            operand = term.astype(jnp.bfloat16)
    fresh_list = [total.astype(jnp.bfloat16)]
    new_orbitals = jnp.stack(fresh_list, axis=0)
    trial_real = trial[:, :nocc].T
    trial_imag = trial[:, nocc:].T
    mixer = jnp.concatenate(
        [
            jnp.concatenate([trial_real, -trial_imag], axis=1),
            jnp.concatenate([trial_imag, trial_real], axis=1),
        ],
        axis=0,
    )
    orbital_rows = lax.all_to_all(new_orbitals, "wide", split_axis=1, concat_axis=0, tiled=True)
    count = orbital_rows.shape[0]
    flat_rows = orbital_rows.reshape(count * rows, 2 * nocc)
    tile_green = jnp.dot(flat_rows, mixer, preferred_element_type=jnp.float32).astype(jnp.bfloat16)
    tile_green = tile_green.reshape(count, rows, 2 * width)
    all_walk = tile_green.shape[0]
    tile_green = (
        tile_green.reshape(all_walk, rows, 2, width)
        .transpose(0, 2, 1, 3)
        .reshape(all_walk * 2, rows * width)
    )
    partial_value = jnp.dot(tile_green, chol_flat.T, preferred_element_type=jnp.float32).reshape(
        all_walk, 2, vectors
    )
    summed = lax.psum(partial_value, "wide")
    force_bias = lax.dynamic_slice_in_dim(
        summed, lax.axis_index("wide") * walk_local, walk_local, 0
    )
    return (new_orbitals, force_bias)


def solution(mesh):
    in_specs = (
        P(("groups", "wide"), None),
        P(None, "wide", None),
        P(("groups", "wide"), None, None),
        P(),
    )
    out_specs = (P(("groups", "wide"), None, None), P(("groups", "wide"), None, None))
    return jax.shard_map(
        per_device, mesh=mesh, in_specs=in_specs, out_specs=out_specs, check_vma=False
    )
```

profile of v0, /device:TPU:8, one launch (start us, length us, event | category | flops | bytes accessed | tf_op | source)
XLA Modules:
  0.0 381.3 jit_solution(17390543338026890626)
XLA Ops:
  7.2 0.0 copy-start.2
  7.2 58.5 %copy.31 = bf16[64,8,64,1024]{3,1,2,0:T(8,128)(2,1)} copy(bf16[64,8,64,1024]{3,2,1,0:T(8,128)(2,1)} %bitcast.19) | data formatting | bytes 134217728
  65.7 0.0 copy-done.2
  65.7 18.9 %all-gather = bf16[16,1,512]{2,1,0:T(2,128)(2,1)S(1)} all-gather(bf16[1,1,512]{2,1,0:T(2,128)(2,1)S(1)} %bitcast.65), channel_id=1, replica_groups=mesh['groups'=2,'wide'=16] {'wide'}, dimensions={0}, use_global_device_ids=true | all-gather | bytes 17408 | tf_op jit(solution)/shard_map/all_gather | solution.py:10
  84.6 22.8 %convolution_convert_fusion = bf16[16,65536]{1,0:T(8,128)(2,1)S(1)} fusion(bf16[512,65536]{1,0:T(8,128)(2,1)} %bitcast.20, bf16[16,1,512]{2,1,0:T(2,128)(2,1)S(1)} %all-gather), kind=kOutput, calls=%fused_computation | convolution fusion | flops 1074790400 | bytes 69222400 | tf_op jit(solution)/shard_map/dot_general | solution.py:13
  107.4 2.5 copy.32
  109.9 0.0 copy-start
  109.9 6.9 %all-to-all-start = ((bf16[16,64,1024]{2,1,0:T(8,128)(2,1)}), bf16[16,64,1024]{2,1,0:T(8,128)(2,1)S(1)}, u32[]{:S(2)}, u32[]{:S(2)}) async-start(bf16[16,64,1024]{2,1,0:T(8,128)(2,1)} %bitcast.62), calls=%async_computation | async-start | bytes 4194304 | tf_op jit(solution)/shard_map/all_to_all | solution.py:17
  116.8 0.0 copy-done
  116.8 0.2 copy.22
  117.0 45.6 %all-to-all-done = bf16[16,64,1024]{2,1,0:T(8,128)(2,1)S(1)} async-done(((bf16[16,64,1024]{2,1,0:T(8,128)(2,1)}), bf16[16,64,1024]{2,1,0:T(8,128)(2,1)S(1)}, u32[]{:S(2)}, u32[]{:S(2)}) %all-to-all-start) | async-done | bytes 2097184 | tf_op jit(solution)/shard_map/all_to_all | solution.py:17
  162.7 0.8 fusion.34
  163.4 0.1 fusion.38
  163.6 0.7 fusion.28
  164.3 0.1 slice_negate_fusion.2
  164.5 0.7 fusion.25
  165.2 0.1 slice_negate_fusion.1
  165.4 0.7 fusion.23
  166.1 0.1 fusion.27
  166.2 0.6 fusion.13
  166.8 0.9 copy.23
  167.6 0.0 copy-start.1
  167.7 0.5 broadcast.24
  168.2 3.8 %reduce = bf16[1024,256]{1,0:T(8,128)(2,1)S(1)} reduce(bf16[1024,1,256]{2,1,0:T(2,128)(2,1)S(1)} %bitcast.63, bf16[]{:T(256)} %broadcast.24), dimensions={1}, to_apply=%bitcast.50.reduce_sub_computation | reduce | bytes 1048578
  172.0 0.9 reshape.121
  172.9 6.4 %all-to-all-start.1 = ((bf16[16,2,8192]{2,1,0:T(2,128)(2,1)}), bf16[16,2,8192]{2,1,0:T(2,128)(2,1)S(1)}, u32[]{:S(2)}, u32[]{:S(2)}) async-start(bf16[16,2,8192]{2,1,0:T(2,128)(2,1)} %reshape.121), calls=%async_computation.1 | async-start | bytes 1048576 | tf_op jit(solution)/shard_map/all_to_all | solution.py:40
  179.3 0.0 all-reduce.2.cloned.1.call-start
  179.3 0.0 copy-done.1
  179.4 13.3 %all-to-all-done.1 = bf16[16,2,8192]{2,1,0:T(2,128)(2,1)S(1)} async-done(((bf16[16,2,8192]{2,1,0:T(2,128)(2,1)}), bf16[16,2,8192]{2,1,0:T(2,128)(2,1)S(1)}, u32[]{:S(2)}, u32[]{:S(2)}) %all-to-all-start.1) | async-done | bytes 524320 | tf_op jit(solution)/shard_map/all_to_all | solution.py:40
  192.8 0.5 reshape.122
  193.3 3.3 convolution_convert_fusion.1
  196.6 7.8 %reshape_reshape.3 = bf16[16,64,2,1024]{3,2,1,0:T(2,128)(2,1)} reshape(bf16[1024,2048]{1,0:T(8,128)(2,1)} %convolution_convert_fusion.1) | data formatting | bytes 8388608 | tf_op jit(solution)/shard_map/reshape;reshape | solution.py:47
  204.3 80.0 %fusion.5 = f32[16,2,512]{2,0,1:T(8,128)} fusion(bf16[512,64,1024]{2,1,0:T(8,128)(2,1)} %param.5, bf16[16,64,2,1024]{3,2,1,0:T(2,128)(2,1)} %reshape_reshape.3), kind=kOutput, calls=%fused_computation.7 | convolution fusion | flops 2147483648 | bytes 71368704 | tf_op jit(solution)/shard_map/dot_general | solution.py:51
  284.3 0.0 all-reduce.2.cloned.1.call-update
  284.3 1.0 copy.26
  285.3 87.8 %all-reduce.2.cloned.1.call-done = f32[16,2,512]{2,0,1:T(8,128)} async-done(((f32[16,2,512]{2,0,1:T(8,128)}), f32[16,2,512]{2,0,1:T(8,128)}) %all-reduce.2.cloned.1.call-update) | async-done | bytes 65552 | tf_op jit(solution)/shard_map/psum | solution.py:54
  373.1 0.8 constant_dynamic-slice_fusion
  373.9 0.6 copy.27
  (3 shorter events, 0.1 us)
Async XLA Ops:
  7.2 58.6 %copy-start.2 = (bf16[1,512]{1,0:T(2,128)(2,1)S(1)}, bf16[1,512]{1,0:T(2,128)(2,1)}, u32[]{:S(2)}) copy-start(bf16[1,512]{1,0:T(2,128)(2,1)} %param.4) | copy-start | bytes 3076
  109.9 6.9 %copy-start = (bf16[1,1024,256]{2,1,0:T(8,128)(2,1)S(1)}, bf16[1,1024,256]{2,1,0:T(8,128)(2,1)}, u32[]{:S(2)}) copy-start(bf16[1,1024,256]{2,1,0:T(8,128)(2,1)} %param.6) | copy-start | bytes 1572868
  109.9 52.8 %all-to-all-start = ((bf16[16,64,1024]{2,1,0:T(8,128)(2,1)}), bf16[16,64,1024]{2,1,0:T(8,128)(2,1)S(1)}, u32[]{:S(2)}, u32[]{:S(2)}) async-start(bf16[16,64,1024]{2,1,0:T(8,128)(2,1)} %bitcast.62), calls=%async_computation | async-start | bytes 4194304 | tf_op jit(solution)/shard_map/all_to_all | solution.py:17
  167.6 11.7 %copy-start.1 = (bf16[1024,256]{1,0:T(8,128)(2,1)S(1)}, bf16[1024,256]{1,0:T(8,128)(2,1)}, u32[]{:S(2)}) copy-start(bf16[1024,256]{1,0:T(8,128)(2,1)} %param.7) | copy-start | bytes 1572868
  172.9 19.8 %all-to-all-start.1 = ((bf16[16,2,8192]{2,1,0:T(2,128)(2,1)}), bf16[16,2,8192]{2,1,0:T(2,128)(2,1)S(1)}, u32[]{:S(2)}, u32[]{:S(2)}) async-start(bf16[16,2,8192]{2,1,0:T(2,128)(2,1)} %reshape.121), calls=%async_computation.1 | async-start | bytes 1048576 | tf_op jit(solution)/shard_map/all_to_all | solution.py:40
  179.3 193.8 %all-reduce.2.cloned.1.call-start = ((), (), s32[]{:S(2)}) async-start(), calls=%async_computation.2 | async-start | bytes 131072 | tf_op jit(solution)/shard_map/psum | solution.py:54
Sparse Core Ops, SparseCore 0:
  284.4 88.6 all-reduce.1
where the time goes:
time: 382 us; the launch traced here: 381 us
  waiting for transfers between devices  147 us (38%)
  matrix products  109 us (29%)
  local copies, waits for them, and re-layouts  74.3 us (19%)
  blocking collectives  18.9 us (5%)
  between operations  14.2 us (4%)
  starting transfers between devices  13.3 us (3%)
  other arithmetic  4.9 us (1%)
    psum x1, waiting for transfers between devices, per_device(): summed = lax.psum(partial_value, 'wide')  87.8 us
    dot_general x1, matrix products, per_device(): jnp.dot(tile_green, chol_flat.T, preferred_element_type=jnp.float32)  80 us
    unnamed x14, local copies, waits for them, and re-layouts  64.8 us
    all_to_all x1, waiting for transfers between devices, per_device(): lax.all_to_all(generator, 'wide', split_axis=0, concat_axis=1, tiled=True)  45.6 us
    dot_general x1, matrix products, per_device(): jnp.dot(all_fields, chol_flat, preferred_element_type=jnp.float32)  22.8 us
    all_gather x1, blocking collectives, per_device(): all_fields = lax.all_gather(fields, 'wide', axis=0, tiled=True)  18.9 us
    all_to_all x1, waiting for transfers between devices, per_device(): lax.all_to_all(new_orbitals, 'wide', split_axis=1, concat_axis=0, tiled=T...  13.3 us
    another operation x1, local copies, waits for them, and re-layouts, per_device(): tile_green.reshape(all_walk, rows, 2, width).transpose(0, 2, 1, 3)  7.78 us
  transfers between devices with their start and end apart: 3, of which 3 were waited for; matrix products, arithmetic and copies ran while one was open for 0% of the time, Pallas kernels for 0%

commit v1 on v0

--- a/solution.py
+++ b/solution.py
@@ -51,7 +51,11 @@
     partial_value = jnp.dot(tile_green, chol_flat.T, preferred_element_type=jnp.float32).reshape(
         all_walk, 2, vectors
     )
-    summed = lax.psum(partial_value, "wide")
+
+    def draw_the_case(array_in, link_axis):
+        return jax.lax.all_gather(array_in, axis_name=link_axis).sum(axis=0)
+
+    summed = draw_the_case(partial_value, "wide")
     force_bias = lax.dynamic_slice_in_dim(
         summed, lax.axis_index("wide") * walk_local, walk_local, 0
     )

time: 382 us -> 333 us (0.87)
  waiting for transfers between devices: 147 us -> 94.9 us
    psum x1 -> x0, waiting for transfers between devices: 87.8 us -> none  [per_device(): summed = lax.psum(partial_value, 'wide')]
    all_gather x0 -> x1, waiting for transfers between devices: none -> 35.9 us  [draw_the_case(): return jax.lax.all_gather(array_in, axis_name=link_axis).sum(axis=0)]
where the time goes in v1:
time: 333 us; the launch traced here: 330 us
  matrix products  109 us (33%)
  waiting for transfers between devices  94.9 us (28%)
  local copies, waits for them, and re-layouts  73.5 us (22%)
  blocking collectives  18.9 us (6%)
  between operations  14.2 us (4%)
  starting transfers between devices  13.3 us (4%)
  other arithmetic  6.23 us (2%)
    dot_general x1, matrix products, per_device(): jnp.dot(tile_green, chol_flat.T, preferred_element_type=jnp.float32)  80 us
    unnamed x14, local copies, waits for them, and re-layouts  64.8 us
    all_to_all x1, waiting for transfers between devices, per_device(): lax.all_to_all(generator, 'wide', split_axis=0, concat_axis=1, tiled=True)  45.6 us
    all_gather x1, waiting for transfers between devices, draw_the_case(): return jax.lax.all_gather(array_in, axis_name=link_axis).sum(axis=0)  35.9 us
    dot_general x1, matrix products, per_device(): jnp.dot(all_fields, chol_flat, preferred_element_type=jnp.float32)  22.8 us
    all_gather x1, blocking collectives, per_device(): all_fields = lax.all_gather(fields, 'wide', axis=0, tiled=True)  18.9 us
    all_to_all x1, waiting for transfers between devices, per_device(): lax.all_to_all(new_orbitals, 'wide', split_axis=1, concat_axis=0, tiled=T...  13.3 us
    another operation x1, local copies, waits for them, and re-layouts, per_device(): tile_green.reshape(all_walk, rows, 2, width).transpose(0, 2, 1, 3)  7.78 us
  transfers between devices with their start and end apart: 3, of which 3 were waited for; matrix products, arithmetic and copies ran while one was open for 0% of the time, Pallas kernels for 0%

profile of v1, /device:TPU:8, one launch (start us, length us, event | category | flops | bytes accessed | tf_op | source)
XLA Modules:
  0.0 330.0 jit_solution(16870788138892243443)
XLA Ops:
  7.2 0.0 copy-start.2
  7.2 58.5 %copy.29 = bf16[64,8,64,1024]{3,1,2,0:T(8,128)(2,1)} copy(bf16[64,8,64,1024]{3,2,1,0:T(8,128)(2,1)} %bitcast.20) | data formatting | bytes 134217728
  65.7 0.0 copy-done.2
  65.7 18.9 %all-gather.1 = bf16[16,1,512]{2,1,0:T(2,128)(2,1)S(1)} all-gather(bf16[1,1,512]{2,1,0:T(2,128)(2,1)S(1)} %bitcast.67), channel_id=1, replica_groups=mesh['groups'=2,'wide'=16] {'wide'}, dimensions={0}, use_global_device_ids=true | all-gather | bytes 17408 | tf_op jit(solution)/shard_map/all_gather | solution.py:10
  84.6 22.8 %convolution_convert_fusion = bf16[16,65536]{1,0:T(8,128)(2,1)S(1)} fusion(bf16[512,65536]{1,0:T(8,128)(2,1)} %bitcast.21, bf16[16,1,512]{2,1,0:T(2,128)(2,1)S(1)} %all-gather.1), kind=kOutput, calls=%fused_computation | convolution fusion | flops 1074790400 | bytes 69222400 | tf_op jit(solution)/shard_map/dot_general | solution.py:13
  107.4 2.5 copy.30
  109.9 0.0 copy-start
  109.9 6.9 %all-to-all-start = ((bf16[16,64,1024]{2,1,0:T(8,128)(2,1)}), bf16[16,64,1024]{2,1,0:T(8,128)(2,1)S(1)}, u32[]{:S(2)}, u32[]{:S(2)}) async-start(bf16[16,64,1024]{2,1,0:T(8,128)(2,1)} %bitcast.63), calls=%async_computation | async-start | bytes 4194304 | tf_op jit(solution)/shard_map/all_to_all | solution.py:17
  116.8 0.0 copy-done
  116.8 0.2 copy.20
  117.0 45.6 %all-to-all-done = bf16[16,64,1024]{2,1,0:T(8,128)(2,1)S(1)} async-done(((bf16[16,64,1024]{2,1,0:T(8,128)(2,1)}), bf16[16,64,1024]{2,1,0:T(8,128)(2,1)S(1)}, u32[]{:S(2)}, u32[]{:S(2)}) %all-to-all-start) | async-done | bytes 2097184 | tf_op jit(solution)/shard_map/all_to_all | solution.py:17
  162.7 0.8 fusion.34
  163.4 0.1 fusion.38
  163.6 0.7 fusion.28
  164.3 0.1 slice_negate_fusion.2
  164.5 0.7 fusion.25
  165.2 0.1 slice_negate_fusion.1
  165.4 0.7 fusion.23
  166.1 0.1 fusion.27
  166.2 0.6 fusion.13
  166.8 0.9 copy.21
  167.7 0.0 copy-start.1
  167.7 0.5 broadcast.24
  168.2 3.8 %reduce = bf16[1024,256]{1,0:T(8,128)(2,1)S(1)} reduce(bf16[1024,1,256]{2,1,0:T(2,128)(2,1)S(1)} %bitcast.64, bf16[]{:T(256)} %broadcast.24), dimensions={1}, to_apply=%bitcast.51.reduce_sub_computation | reduce | bytes 1048578
  172.0 0.9 reshape.124
  172.9 6.4 %all-to-all-start.1 = ((bf16[16,2,8192]{2,1,0:T(2,128)(2,1)}), bf16[16,2,8192]{2,1,0:T(2,128)(2,1)S(1)}, u32[]{:S(2)}, u32[]{:S(2)}) async-start(bf16[16,2,8192]{2,1,0:T(2,128)(2,1)} %reshape.124), calls=%async_computation.1 | async-start | bytes 1048576 | tf_op jit(solution)/shard_map/all_to_all | solution.py:40
  179.3 0.0 all-gather.4.cloned.1.call-start
  179.3 0.0 copy-done.1
  179.4 13.3 %all-to-all-done.1 = bf16[16,2,8192]{2,1,0:T(2,128)(2,1)S(1)} async-done(((bf16[16,2,8192]{2,1,0:T(2,128)(2,1)}), bf16[16,2,8192]{2,1,0:T(2,128)(2,1)S(1)}, u32[]{:S(2)}, u32[]{:S(2)}) %all-to-all-start.1) | async-done | bytes 524320 | tf_op jit(solution)/shard_map/all_to_all | solution.py:40
  192.8 0.5 reshape.125
  193.3 3.3 convolution_convert_fusion.1
  196.6 7.8 %reshape_reshape.3 = bf16[16,64,2,1024]{3,2,1,0:T(2,128)(2,1)} reshape(bf16[1024,2048]{1,0:T(8,128)(2,1)} %convolution_convert_fusion.1) | data formatting | bytes 8388608 | tf_op jit(solution)/shard_map/reshape;reshape | solution.py:47
  204.4 80.0 %fusion.5 = f32[16,2,512]{2,0,1:T(8,128)} fusion(bf16[512,64,1024]{2,1,0:T(8,128)(2,1)} %param.5, bf16[16,64,2,1024]{3,2,1,0:T(2,128)(2,1)} %reshape_reshape.3), kind=kOutput, calls=%fused_computation.7 | convolution fusion | flops 2147483648 | bytes 71368704 | tf_op jit(solution)/shard_map/dot_general | solution.py:51
  284.3 0.0 all-gather.4.cloned.1.call-update
  284.4 1.0 copy.24
  285.4 35.9 %all-gather.4.cloned.1.call-done = f32[256,2,512]{2,0,1:T(8,128)} async-done(((f32[16,2,512]{2,0,1:T(8,128)}), f32[256,2,512]{2,0,1:T(8,128)}) %all-gather.4.cloned.1.call-update) | async-done | bytes 1048592 | tf_op jit(solution)/shard_map/all_gather | solution.py:56
  321.3 1.3 reduce_sum.9
  322.6 0.6 copy.25
  (4 shorter events, 0.1 us)
Async XLA Ops:
  7.2 58.6 %copy-start.2 = (bf16[1,512]{1,0:T(2,128)(2,1)S(1)}, bf16[1,512]{1,0:T(2,128)(2,1)}, u32[]{:S(2)}) copy-start(bf16[1,512]{1,0:T(2,128)(2,1)} %param.4) | copy-start | bytes 3076
  109.9 6.9 %copy-start = (bf16[1,1024,256]{2,1,0:T(8,128)(2,1)S(1)}, bf16[1,1024,256]{2,1,0:T(8,128)(2,1)}, u32[]{:S(2)}) copy-start(bf16[1,1024,256]{2,1,0:T(8,128)(2,1)} %param.6) | copy-start | bytes 1572868
  109.9 52.8 %all-to-all-start = ((bf16[16,64,1024]{2,1,0:T(8,128)(2,1)}), bf16[16,64,1024]{2,1,0:T(8,128)(2,1)S(1)}, u32[]{:S(2)}, u32[]{:S(2)}) async-start(bf16[16,64,1024]{2,1,0:T(8,128)(2,1)} %bitcast.63), calls=%async_computation | async-start | bytes 4194304 | tf_op jit(solution)/shard_map/all_to_all | solution.py:17
  167.7 11.7 %copy-start.1 = (bf16[1024,256]{1,0:T(8,128)(2,1)S(1)}, bf16[1024,256]{1,0:T(8,128)(2,1)}, u32[]{:S(2)}) copy-start(bf16[1024,256]{1,0:T(8,128)(2,1)} %param.7) | copy-start | bytes 1572868
  172.9 19.8 %all-to-all-start.1 = ((bf16[16,2,8192]{2,1,0:T(2,128)(2,1)}), bf16[16,2,8192]{2,1,0:T(2,128)(2,1)S(1)}, u32[]{:S(2)}, u32[]{:S(2)}) async-start(bf16[16,2,8192]{2,1,0:T(2,128)(2,1)} %reshape.124), calls=%async_computation.1 | async-start | bytes 1048576 | tf_op jit(solution)/shard_map/all_to_all | solution.py:40
  179.3 142.0 %all-gather.4.cloned.1.call-start = ((), (), s32[]{:S(2)}) async-start(), calls=%async_computation.2 | async-start | bytes 1114112 | tf_op jit(solution)/shard_map/all_gather | solution.py:56
Sparse Core Ops, SparseCore 0:
  284.5 36.7 all-gather.3
